TPU v7x, 32 devices: a whole 2x2x4 slice. The times are simulated.
32 devices in a mesh: seq: 4 (over y, x), head: 8 (over z, core).
Axes of the slice: x: 2, y: 2, z: 4, core: 2. Of those that a mesh axis runs over, the one named last changes fastest.
Arguments:
- sequence_activity: bfloat16 [2, 2048, 4096], P(None, 'seq', 'head'), may hold values from -6 to 6
- lookup_mapping_tensor: bfloat16 [4096, 8, 768], P(None, 'head'), may hold values from -1 to 1, as said below
- stepsize_mapping_matrix: bfloat16 [4096, 8], P(None, 'head'), may hold values from -0.09375 to 0.09375
- logit_sharpness: float32 [8], P('head'), may hold values from 4 to 120
- adapter_gain_vector: float32 [8, 256], P('head'), may hold values from 0.1 to 1.9
- starting_inner_left_matrix: float32 [8, 256, 512], P('head'), may hold values from -0.375 to 0.375
- starting_inner_right_matrix: float32 [8, 512, 256], P('head'), may hold values from -0.25 to 0.25
- final_mixing_matrix: bfloat16 [8, 256, 4096], P('head'), may hold values from -0.125 to 0.125
Outputs:
- mixed: bfloat16 [2, 2048, 4096], P(None, 'seq', 'head')
Inputs may be any that keep to these rules, and one draw needn't show every extreme that they name: `lookup_mapping_tensor`: entries of order 1 / sqrt(4096).
All inputs are finite; a program needn't handle non-finite values.
Results may differ from a plain program's by a relative error of at most 0.02.
Values may be sent and summed in bfloat16 or wider, within the bound.
No kernel may reach another device: no remote copies, remote signals or barrier semaphores. Data moves between devices by JAX's collectives and lax.ppermute only.
A program may use at most 64 MiB of HBM per device.

v0:
```python
import jax
import jax.numpy as jnp
from jax import lax
from jax.sharding import PartitionSpec as P

WIN = 2048
NS_STEPS = 3
update_rate = 0.3


def shifted(block, axis, distance):
    devices = range(lax.axis_size(axis))
    route = [(i - distance, i) for i in devices if i - distance in devices]
    return lax.ppermute(block, axis, route)


def orthogonalize(update):
    scale = lax.rsqrt(jnp.sum(update * update) + 1e-06)
    current = update * scale
    for sweep in range(NS_STEPS):
        if current.shape[0] <= current.shape[1]:
            gram = jnp.dot(current, current.T, precision=lax.Precision.HIGHEST)
            current = 1.5 * current - 0.5 * jnp.dot(gram, current, precision=lax.Precision.HIGHEST)
        else:
            gram = jnp.dot(current.T, current, precision=lax.Precision.HIGHEST)
            current = 1.5 * current - 0.5 * jnp.dot(current, gram, precision=lax.Precision.HIGHEST)
    return current


def fast_group(weight_in, weight_out, keys, weighted, query_rows):
    in_half = weight_in.astype(jnp.bfloat16)
    out_half = weight_out.astype(jnp.bfloat16)
    hidden = jnp.dot(keys, in_half, preferred_element_type=jnp.float32)
    gating = jax.nn.sigmoid(hidden)
    activated = (hidden * gating).astype(jnp.bfloat16)
    grad_out = jnp.dot(activated.T, weighted, preferred_element_type=jnp.float32)
    backward = jnp.dot(weighted, out_half.T, preferred_element_type=jnp.float32)
    slopes = (backward * gating * (1.0 + hidden * (1.0 - gating))).astype(jnp.bfloat16)
    grad_in = jnp.dot(keys.T, slopes, preferred_element_type=jnp.float32)
    new_in = weight_in + update_rate * orthogonalize(grad_in)
    new_out = weight_out + update_rate * orthogonalize(grad_out)
    query_hidden = jnp.dot(
        query_rows, new_in.astype(jnp.bfloat16), preferred_element_type=jnp.float32
    )
    query_act = jax.nn.silu(query_hidden).astype(jnp.bfloat16)
    fast = jnp.dot(query_act, new_out.astype(jnp.bfloat16), preferred_element_type=jnp.float32)
    return (new_in, new_out, fast)


def prepare(projected, rate_col, count_seqs):
    head_dim = projected.shape[1] // 3
    query_rows = projected[:, :head_dim]
    keys = projected[:, head_dim : 2 * head_dim]
    values = projected[:, 2 * head_dim :]
    query_norm = (
        query_rows * lax.rsqrt(jnp.sum(query_rows * query_rows, axis=1, keepdims=True) + 1e-06)
    ).astype(jnp.bfloat16)
    key_norm = (keys * lax.rsqrt(jnp.sum(keys * keys, axis=1, keepdims=True) + 1e-06)).astype(
        jnp.bfloat16
    )
    value_half = values.astype(jnp.bfloat16)
    weighted = (jax.nn.softplus(rate_col) * values).astype(jnp.bfloat16)
    return (
        query_norm.reshape(count_seqs, -1, head_dim),
        key_norm.reshape(count_seqs, -1, head_dim),
        value_half.reshape(count_seqs, -1, head_dim),
        weighted.reshape(count_seqs, -1, head_dim),
    )


def attend_window(query_rows, keys, values, scale, start):
    count = query_rows.shape[1]
    window = keys.shape[1] - count
    scores = scale * jnp.einsum(
        "sqd,skd->sqk", query_rows, keys, preferred_element_type=jnp.float32
    )
    row_pos = lax.broadcasted_iota(jnp.int32, (count, count + window), 0)
    col_pos = lax.broadcasted_iota(jnp.int32, (count, count + window), 1)
    valid = (col_pos >= row_pos) & (col_pos <= row_pos + window) & (col_pos + start >= window)
    scores = jnp.where(valid[None], scores, -1e30)
    highest = jnp.max(scores, axis=2, keepdims=True)
    weights = jnp.exp(scores - highest)
    probs = (weights / jnp.sum(weights, axis=2, keepdims=True)).astype(jnp.bfloat16)
    return jnp.einsum("sqk,skd->sqd", probs, values, preferred_element_type=jnp.float32)


def combine(attended_output, fast, gain):
    normed = fast * lax.rsqrt(jnp.mean(fast * fast, axis=-1, keepdims=True) + 1e-05) * gain
    return (attended_output + normed).astype(jnp.bfloat16)


def body(
    sequence_activity,
    lookup_mapping_tensor,
    stepsize_mapping_matrix,
    logit_sharpness,
    adapter_gain_vector,
    starting_inner_left_matrix,
    starting_inner_right_matrix,
    final_mixing_matrix,
):
    seqs, head_group, local_width = sequence_activity.shape
    total_rows = seqs * head_group
    flattened = sequence_activity.reshape(total_rows, local_width)
    weights_in = lookup_mapping_tensor.reshape(
        lookup_mapping_tensor.shape[0], lookup_mapping_tensor.shape[2]
    )
    head_dim = weights_in.shape[1] // 3
    piece = lax.all_gather(flattened, "head", axis=1, tiled=True)
    projected = jnp.dot(piece, weights_in, preferred_element_type=jnp.float32)
    rate_col = jnp.dot(piece, stepsize_mapping_matrix, preferred_element_type=jnp.float32)
    query_rows, keys, values, weighted = prepare(projected, rate_col, seqs)
    token_position = lax.axis_index("seq")
    length = lax.axis_size("seq")
    reach = WIN // head_group
    hops = min(reach, length - 1)
    empty = jnp.zeros_like(keys)
    earlier = []
    current = (keys, values)
    for distance in range(hops):
        current = shifted((current[0], current[1]), "seq", 1)
        earlier.insert(0, current)
    for missing in range(reach - hops):
        earlier.insert(0, (empty, empty))
    windowed_key_rows = jnp.concatenate([pair[0] for pair in earlier] + [keys], axis=1)
    windowed_value_rows = jnp.concatenate([pair[1] for pair in earlier] + [values], axis=1)
    attended_output = attend_window(
        query_rows,
        windowed_key_rows,
        windowed_value_rows,
        logit_sharpness[0],
        token_position * head_group,
    )
    start_in = starting_inner_left_matrix[0]
    start_out = starting_inner_right_matrix[0]

    def turn(step, carry):
        held_in, held_out, fast_all = carry
        which = step // length
        live = step % length == token_position
        which = jnp.clip(which, 0, seqs - 1)
        use_in = jnp.where(token_position == 0, start_in, held_in)
        use_out = jnp.where(token_position == 0, start_out, held_out)
        block_keys = lax.dynamic_index_in_dim(keys, which, 0, keepdims=False)
        block_weighted = lax.dynamic_index_in_dim(weighted, which, 0, keepdims=False)
        block_queries = lax.dynamic_index_in_dim(query_rows, which, 0, keepdims=False)

        def working():
            return fast_group(use_in, use_out, block_keys, block_weighted, block_queries)

        def resting():
            return (use_in, use_out, jnp.zeros((head_group, head_dim), jnp.float32))

        new_in, new_out, fast = lax.cond(live, working, resting)
        stored = lax.dynamic_update_index_in_dim(fast_all, fast, which, 0)
        fast_all = jnp.where(live, stored, fast_all)
        sent_in, sent_out = shifted((new_in, new_out), "seq", 1)
        return (sent_in, sent_out, fast_all)

    turns = seqs * length
    carried = (start_in, start_out, jnp.zeros((seqs, head_group, head_dim), jnp.float32))
    carried = lax.fori_loop(0, turns, turn, carried)
    head_out = combine(attended_output, carried[2], adapter_gain_vector[0]).reshape(
        total_rows, head_dim
    )
    columns = lax.all_to_all(final_mixing_matrix, "head", split_axis=2, concat_axis=0, tiled=True)
    columns = columns.reshape(-1, columns.shape[2])
    result = jnp.dot(
        lax.all_gather(head_out, "head", axis=1, tiled=True),
        columns,
        preferred_element_type=jnp.float32,
    )
    return result.astype(jnp.bfloat16).reshape(seqs, head_group, -1)


def solution(mesh):
    in_specs = (
        P(None, "seq", "head"),
        P(None, "head", None),
        P(None, "head"),
        P("head"),
        P("head", None),
        P("head", None, None),
        P("head", None, None),
        P("head", None, None),
    )
    out_specs = P(None, "seq", "head")
    return jax.shard_map(body, mesh=mesh, in_specs=in_specs, out_specs=out_specs, check_vma=False)
```

profile of v0, /device:TPU:0, one launch (start us, length us, event | category | flops | bytes accessed | tf_op | source)
XLA Modules:
  0.0 614.8 jit_solution(14468545543711807388)
XLA Ops:
  7.3 86.4 %all-gather.3.cloned.1.call-done = bf16[1024,4096]{1,0:T(8,128)(2,1)} async-done(((bf16[1024,512]{1,0:T(8,128)(2,1)}), bf16[1024,4096]{1,0:T(8,128)(2,1)}) %all-gather.3.cloned.1.call-update) | async-done | bytes 8388624 | tf_op jit(solution)/shard_map/all_gather | solution.py:109
  93.7 5.8 fusion.86
  99.6 9.0 %fusion.61 = f32[1024,768]{1,0:T(8,128)S(1)} fusion(bf16[1024,4096]{1,0:T(8,128)(2,1)S(1)} %copy-done.3, bf16[4096,1,768]{2,0,1:T(8,128)(2,1)} %param.13), kind=kOutput, calls=%fused_computation.72 | convolution fusion | flops 6442450944 | bytes 17825792 | tf_op jit(solution)/shard_map/dot_general | solution.py:110
  143.1 5.9 collective-permute-done.3
  155.4 297.8 %while.19 = (s32[]{:T(128)}, f32[256,512]{1,0:T(8,128)}, f32[512,256]{1,0:T(8,128)}, f32[2,512,256]{2,1,0:T(8,128)}, s32[]{:T(128)}, /*index=5*/pred[]{:T(512)},...) while((s32[]{:T(128)}, f32[256,512]{1,0:T(8,128)}, ...), condition=%wide.region_9.10_spmd, body=%wide.region_4.9_spmd.sunk | while | flops 5647237120 | bytes 32771136 | solution.py:162
  157.6 17.1 %conditional.2 = (f32[256,512]{1,0:T(8,128)S(1)}, f32[512,256]{1,0:T(8,128)S(1)}, f32[1,512,256]{2,1,0:T(8,128)S(1)}) conditional(s32[]{:T(128)} %convert_element_type.110, (f32[256,512]{1,0:T(8,128)S(1)}, f32[512,256]{1,0:T(8,128)S(1)}) %tuple.60, (bf16[2,512,256]{2,1,0:T(8,128)(2,1)}, s32[]{:T(128)}, bf16[2,512,256]{2,1,0:T(8,128)(2,1)}, ...), branch_computations={%region_5.5_spmd, %region_6.8_spmd} | conditional | flops 5646843904 | bytes 23857272 | solution.py:154
  180.8 7.5 %collective-permute-done = f32[256,512]{1,0:T(8,128)} collective-permute-done((f32[256,512]{1,0:T(8,128)S(1)}, f32[256,512]{1,0:T(8,128)}, u32[]{:S(2)}, u32[]{:S(2)}) %collective-permute-start) | collective-permute-done | bytes 524320 | tf_op jit(solution)/shard_map/while/body/eval_jaxpr/ppermute | solution.py:14
  188.3 8.9 %collective-permute-done.1 = f32[512,256]{1,0:T(8,128)} collective-permute-done((f32[512,256]{1,0:T(8,128)S(1)}, f32[512,256]{1,0:T(8,128)}, u32[]{:S(2)}, u32[]{:S(2)}) %collective-permute-start.1) | collective-permute-done | bytes 524320 | tf_op jit(solution)/shard_map/while/body/eval_jaxpr/ppermute | solution.py:14
  199.5 22.3 %collective-permute-start = (f32[256,512]{1,0:T(8,128)S(1)}, f32[256,512]{1,0:T(8,128)}, u32[]{:S(2)}, u32[]{:S(2)}) collective-permute-start(f32[256,512]{1,0:T(8,128)S(1)} %get-tuple-element.431), channel_id=1, source_target_pairs={{0,8},{8,16},{16,24},{1,9},{9,17},{17,25},{2,10},{10,18},{18,26},{... | collective-permute-start | bytes 1572872 | tf_op jit(solution)/shard_map/while/body/eval_jaxpr/ppermute | solution.py:14
  225.8 7.5 %collective-permute-done = f32[256,512]{1,0:T(8,128)} collective-permute-done((f32[256,512]{1,0:T(8,128)S(1)}, f32[256,512]{1,0:T(8,128)}, u32[]{:S(2)}, u32[]{:S(2)}) %collective-permute-start) | collective-permute-done | bytes 524320 | tf_op jit(solution)/shard_map/while/body/eval_jaxpr/ppermute | solution.py:14
  233.3 8.1 %collective-permute-done.1 = f32[512,256]{1,0:T(8,128)} collective-permute-done((f32[512,256]{1,0:T(8,128)S(1)}, f32[512,256]{1,0:T(8,128)}, u32[]{:S(2)}, u32[]{:S(2)}) %collective-permute-start.1) | collective-permute-done | bytes 524320 | tf_op jit(solution)/shard_map/while/body/eval_jaxpr/ppermute | solution.py:14
  249.0 20.1 %collective-permute-start.1 = (f32[512,256]{1,0:T(8,128)S(1)}, f32[512,256]{1,0:T(8,128)}, u32[]{:S(2)}, u32[]{:S(2)}) collective-permute-start(f32[512,256]{1,0:T(8,128)S(1)} %get-tuple-element.432), channel_id=1, source_target_pairs={{0,8},{8,16},{16,24},{1,9},{9,17},{17,25},{2,10},{10,18},{18,26},{... | collective-permute-start | bytes 1572872 | tf_op jit(solution)/shard_map/while/body/eval_jaxpr/ppermute | solution.py:14
  271.0 5.6 collective-permute-done.1
  278.9 12.3 %collective-permute-start = (f32[256,512]{1,0:T(8,128)S(1)}, f32[256,512]{1,0:T(8,128)}, u32[]{:S(2)}, u32[]{:S(2)}) collective-permute-start(f32[256,512]{1,0:T(8,128)S(1)} %get-tuple-element.431), channel_id=1, source_target_pairs={{0,8},{8,16},{16,24},{1,9},{9,17},{17,25},{2,10},{10,18},{18,26},{... | collective-permute-start | bytes 1572872 | tf_op jit(solution)/shard_map/while/body/eval_jaxpr/ppermute | solution.py:14
  291.2 5.4 collective-permute-start.1
  302.7 6.7 %collective-permute-done.1 = f32[512,256]{1,0:T(8,128)} collective-permute-done((f32[512,256]{1,0:T(8,128)S(1)}, f32[512,256]{1,0:T(8,128)}, u32[]{:S(2)}, u32[]{:S(2)}) %collective-permute-start.1) | collective-permute-done | bytes 524320 | tf_op jit(solution)/shard_map/while/body/eval_jaxpr/ppermute | solution.py:14
  311.6 17.0 %conditional.2 = (f32[256,512]{1,0:T(8,128)S(1)}, f32[512,256]{1,0:T(8,128)S(1)}, f32[1,512,256]{2,1,0:T(8,128)S(1)}) conditional(s32[]{:T(128)} %convert_element_type.110, (f32[256,512]{1,0:T(8,128)S(1)}, f32[512,256]{1,0:T(8,128)S(1)}) %tuple.60, (bf16[2,512,256]{2,1,0:T(8,128)(2,1)}, s32[]{:T(128)}, bf16[2,512,256]{2,1,0:T(8,128)(2,1)}, ...), branch_computations={%region_5.5_spmd, %region_6.8_spmd} | conditional | flops 5646843904 | bytes 23857272 | solution.py:154
  330.7 5.7 collective-permute-start.1
  342.3 6.1 collective-permute-done.1
  350.7 23.5 %collective-permute-start = (f32[256,512]{1,0:T(8,128)S(1)}, f32[256,512]{1,0:T(8,128)}, u32[]{:S(2)}, u32[]{:S(2)}) collective-permute-start(f32[256,512]{1,0:T(8,128)S(1)} %get-tuple-element.431), channel_id=1, source_target_pairs={{0,8},{8,16},{16,24},{1,9},{9,17},{17,25},{2,10},{10,18},{18,26},{... | collective-permute-start | bytes 1572872 | tf_op jit(solution)/shard_map/while/body/eval_jaxpr/ppermute | solution.py:14
  378.1 7.1 %collective-permute-done = f32[256,512]{1,0:T(8,128)} collective-permute-done((f32[256,512]{1,0:T(8,128)S(1)}, f32[256,512]{1,0:T(8,128)}, u32[]{:S(2)}, u32[]{:S(2)}) %collective-permute-start) | collective-permute-done | bytes 524320 | tf_op jit(solution)/shard_map/while/body/eval_jaxpr/ppermute | solution.py:14
  385.3 5.6 collective-permute-done.1
  398.5 20.1 %collective-permute-start.1 = (f32[512,256]{1,0:T(8,128)S(1)}, f32[512,256]{1,0:T(8,128)}, u32[]{:S(2)}, u32[]{:S(2)}) collective-permute-start(f32[512,256]{1,0:T(8,128)S(1)} %get-tuple-element.432), channel_id=1, source_target_pairs={{0,8},{8,16},{16,24},{1,9},{9,17},{17,25},{2,10},{10,18},{18,26},{... | collective-permute-start | bytes 1572872 | tf_op jit(solution)/shard_map/while/body/eval_jaxpr/ppermute | solution.py:14
  426.8 11.0 %collective-permute-start = (f32[256,512]{1,0:T(8,128)S(1)}, f32[256,512]{1,0:T(8,128)}, u32[]{:S(2)}, u32[]{:S(2)}) collective-permute-start(f32[256,512]{1,0:T(8,128)S(1)} %get-tuple-element.431), channel_id=1, source_target_pairs={{0,8},{8,16},{16,24},{1,9},{9,17},{17,25},{2,10},{10,18},{18,26},{... | collective-permute-start | bytes 1572872 | tf_op jit(solution)/shard_map/while/body/eval_jaxpr/ppermute | solution.py:14
  447.5 5.6 collective-permute-done.1
  454.8 14.5 %collective-permute-start.7 = (bf16[2,512,256]{2,1,0:T(8,128)(2,1)}, bf16[2,512,256]{2,1,0:T(8,128)(2,1)S(1)}, u32[]{:S(2)}, u32[]{:S(2)}) collective-permute-start(bf16[2,512,256]{2,1,0:T(8,128)(2,1)} %collective-permute-done.6), channel_id=1, source_target_pairs={{0,8},{8,16},{16,24},{1,9},{9,17},{17,25},{2,10},{10,18},{18,26},{... | collective-permute-start | bytes 1572872 | tf_op jit(solution)/shard_map/ppermute | solution.py:14
  479.8 5.6 fusion.81
  485.5 8.3 %fusion.70 = bf16[2,512,256]{2,1,0:T(8,128)(2,1)} fusion(bf16[2,2560,256]{2,1,0:T(8,128)(2,1)} %copy-done.14, f32[2,512]{1,0:T(2,128)S(1)} %fusion.81, f32[2,512,256]{2,1,0:T(8,128)S(1)} %copy-done.2, f32[256]{0:T(256)S(1)} %bitcast.85, f32[2,512]{1,0:T(2,128)S(1)} %add_rsqrt_fusion, f32[]{:T(128)} %bitcast.72, pred[512,2560]{1,0:T(8,128)(4,1)} %fusion.67, ...), kind=kOutput, calls=%fused_computation.84 | convolution fusion | flops 2698513920 | bytes 8659972 | tf_op jit(solution)/shard_map/sqk,skd->sqd/dot_general | solution.py:84
  493.8 7.3 %copy.11 = bf16[1,256,4096]{1,0,2:T(2,128)(2,1)} copy(bf16[1,256,4096]{2,1,0:T(8,128)(2,1)S(1)} %copy-done.5) | data formatting | bytes 4194304 | tf_op args[7]
  501.7 21.6 %reduce = bf16[4096,256]{1,0:T(8,128)(2,1)S(1)} reduce(bf16[4096,1,256]{2,1,0:T(2,128)(2,1)} %bitcast.74, bf16[]{:T(256)} %broadcast.150), dimensions={1}, to_apply=%bitcast.36.reduce_sub_computation | reduce | bytes 4194306
  526.6 65.8 %all_to_all.15 = bf16[8,2,65536]{2,1,0:T(2,128)(2,1)S(1)} all-to-all(bf16[8,2,65536]{2,1,0:T(2,128)(2,1)} %reshape.120), channel_id=1, replica_groups=mesh['seq'=4,'head'=8] {'head'}, dimensions={0} | all-to-all | bytes 4194304 | tf_op jit(solution)/shard_map/all_to_all | solution.py:166
  601.8 6.2 %convolution_convert_fusion = bf16[1024,512]{1,0:T(8,128)(2,1)} fusion(bf16[1024,2048]{1,0:T(8,128)(2,1)} %all-gather.5.cloned.1.call-done, bf16[2048,512]{1,0:T(8,128)(2,1)} %bitcast.77), kind=kOutput, calls=%fused_computation.82 | convolution fusion | flops 2148007936 | bytes 7340032 | tf_op jit(solution)/shard_map/dot_general | solution.py:168
  (159 shorter events, 171.7 us)
Async XLA Ops:
  6.5 87.2 %copy-start = (bf16[4096,1]{0,1:T(2,128)(2,1)S(1)}, bf16[4096,1]{0,1:T(2,128)(2,1)}, u32[]{:S(2)}) copy-start(bf16[4096,1]{0,1:T(2,128)(2,1)} %param.14) | copy-start | bytes 24580
  6.5 87.2 %all-gather.3.cloned.1.call-start = ((), (), s32[]{:S(2)}) async-start(), calls=%async_computation.1 | async-start | bytes 9437184 | tf_op jit(solution)/shard_map/all_gather | solution.py:109
  7.3 594.5 %all-gather.5.cloned.1.call-start = ((), (), s32[]{:S(2)}) async-start(), calls=%async_computation.2 | async-start | bytes 4718592 | tf_op jit(solution)/shard_map/all_gather | solution.py:169
  110.7 16.0 %collective-permute-start.2 = (bf16[2,512,256]{2,1,0:T(8,128)(2,1)}, bf16[2,512,256]{2,1,0:T(8,128)(2,1)S(1)}, u32[]{:S(2)}, u32[]{:S(2)}) collective-permute-start(bf16[2,512,256]{2,1,0:T(8,128)(2,1)} %bitcast.8), channel_id=1, source_target_pairs={{0,8},{8,16},{16,24},{1,9},{9,17},{17,25},{2,10},{10,18},{18,26},{... | collective-permute-start | bytes 1572872 | tf_op jit(solution)/shard_map/ppermute | solution.py:14
  121.4 33.9 %copy-start.6 = (bf16[1024,256]{1,0:T(8,128)(2,1)}, bf16[1024,256]{1,0:T(8,128)(2,1)S(1)}, u32[]{:S(2)}) copy-start(bf16[1024,256]{1,0:T(8,128)(2,1)S(1)} %slice.21) | copy-start | bytes 1572868
  121.4 16.4 %collective-permute-start.5 = (bf16[2,512,256]{2,1,0:T(8,128)(2,1)S(1)}, bf16[2,512,256]{2,1,0:T(8,128)(2,1)}, u32[]{:S(2)}, u32[]{:S(2)}) collective-permute-start(bf16[2,512,256]{2,1,0:T(8,128)(2,1)S(1)} %bitcast.78), channel_id=1, source_target_pairs={{0,8},{8,16},{16,24},{1,9},{9,17},{17,25},{2,10},{10,18},{18,26},{... | collective-permute-start | bytes 1572872 | tf_op jit(solution)/shard_map/ppermute | solution.py:14
  126.7 28.7 %copy-start.9 = (bf16[2,512,256]{2,1,0:T(8,128)(2,1)}, bf16[2,512,256]{2,1,0:T(8,128)(2,1)S(1)}, u32[]{:S(2)}) copy-start(bf16[2,512,256]{2,1,0:T(8,128)(2,1)S(1)} %collective-permute-done.2) | copy-start | bytes 1572868
  126.7 22.4 %collective-permute-start.3 = (bf16[2,512,256]{2,1,0:T(8,128)(2,1)S(1)}, bf16[2,512,256]{2,1,0:T(8,128)(2,1)}, u32[]{:S(2)}, u32[]{:S(2)}) collective-permute-start(bf16[2,512,256]{2,1,0:T(8,128)(2,1)S(1)} %collective-permute-done.2), channel_id=1, source_target_pairs={{0,8},{8,16},{16,24},{1,9},{9,17},{17,25},{2,10},{10,18},{18,26},{... | collective-permute-start | bytes 1572872 | tf_op jit(solution)/shard_map/ppermute | solution.py:14
  137.8 316.9 %collective-permute-start.6 = (bf16[2,512,256]{2,1,0:T(8,128)(2,1)}, bf16[2,512,256]{2,1,0:T(8,128)(2,1)}, u32[]{:S(2)}, u32[]{:S(2)}) collective-permute-start(bf16[2,512,256]{2,1,0:T(8,128)(2,1)} %collective-permute-done.5), channel_id=1, source_target_pairs={{0,8},{8,16},{16,24},{1,9},{9,17},{17,25},{2,10},{10,18},{18,26},{... | collective-permute-start | bytes 1572872 | tf_op jit(solution)/shard_map/ppermute | solution.py:14
  149.0 320.3 %collective-permute-start.4 = (bf16[2,512,256]{2,1,0:T(8,128)(2,1)}, bf16[2,512,256]{2,1,0:T(8,128)(2,1)}, u32[]{:S(2)}, u32[]{:S(2)}) collective-permute-start(bf16[2,512,256]{2,1,0:T(8,128)(2,1)} %collective-permute-done.3), channel_id=1, source_target_pairs={{0,8},{8,16},{16,24},{1,9},{9,17},{17,25},{2,10},{10,18},{18,26},{... | collective-permute-start | bytes 1572872 | tf_op jit(solution)/shard_map/ppermute | solution.py:14
  174.7 13.6 %collective-permute-start = (f32[256,512]{1,0:T(8,128)S(1)}, f32[256,512]{1,0:T(8,128)}, u32[]{:S(2)}, u32[]{:S(2)}) collective-permute-start(f32[256,512]{1,0:T(8,128)S(1)} %get-tuple-element.431), channel_id=1, source_target_pairs={{0,8},{8,16},{16,24},{1,9},{9,17},{17,25},{2,10},{10,18},{18,26},{... | collective-permute-start | bytes 1572872 | tf_op jit(solution)/shard_map/while/body/eval_jaxpr/ppermute | solution.py:14
  176.8 20.4 %collective-permute-start.1 = (f32[512,256]{1,0:T(8,128)S(1)}, f32[512,256]{1,0:T(8,128)}, u32[]{:S(2)}, u32[]{:S(2)}) collective-permute-start(f32[512,256]{1,0:T(8,128)S(1)} %get-tuple-element.432), channel_id=1, source_target_pairs={{0,8},{8,16},{16,24},{1,9},{9,17},{17,25},{2,10},{10,18},{18,26},{... | collective-permute-start | bytes 1572872 | tf_op jit(solution)/shard_map/while/body/eval_jaxpr/ppermute | solution.py:14
  199.5 33.8 %collective-permute-start = (f32[256,512]{1,0:T(8,128)S(1)}, f32[256,512]{1,0:T(8,128)}, u32[]{:S(2)}, u32[]{:S(2)}) collective-permute-start(f32[256,512]{1,0:T(8,128)S(1)} %get-tuple-element.431), channel_id=1, source_target_pairs={{0,8},{8,16},{16,24},{1,9},{9,17},{17,25},{2,10},{10,18},{18,26},{... | collective-permute-start | bytes 1572872 | tf_op jit(solution)/shard_map/while/body/eval_jaxpr/ppermute | solution.py:14
  221.8 19.6 %collective-permute-start.1 = (f32[512,256]{1,0:T(8,128)S(1)}, f32[512,256]{1,0:T(8,128)}, u32[]{:S(2)}, u32[]{:S(2)}) collective-permute-start(f32[512,256]{1,0:T(8,128)S(1)} %get-tuple-element.432), channel_id=1, source_target_pairs={{0,8},{8,16},{16,24},{1,9},{9,17},{17,25},{2,10},{10,18},{18,26},{... | collective-permute-start | bytes 1572872 | tf_op jit(solution)/shard_map/while/body/eval_jaxpr/ppermute | solution.py:14
  243.7 27.3 %collective-permute-start = (f32[256,512]{1,0:T(8,128)S(1)}, f32[256,512]{1,0:T(8,128)}, u32[]{:S(2)}, u32[]{:S(2)}) collective-permute-start(f32[256,512]{1,0:T(8,128)S(1)} %get-tuple-element.431), channel_id=1, source_target_pairs={{0,8},{8,16},{16,24},{1,9},{9,17},{17,25},{2,10},{10,18},{18,26},{... | collective-permute-start | bytes 1572872 | tf_op jit(solution)/shard_map/while/body/eval_jaxpr/ppermute | solution.py:14
  249.0 27.6 %collective-permute-start.1 = (f32[512,256]{1,0:T(8,128)S(1)}, f32[512,256]{1,0:T(8,128)}, u32[]{:S(2)}, u32[]{:S(2)}) collective-permute-start(f32[512,256]{1,0:T(8,128)S(1)} %get-tuple-element.432), channel_id=1, source_target_pairs={{0,8},{8,16},{16,24},{1,9},{9,17},{17,25},{2,10},{10,18},{18,26},{... | collective-permute-start | bytes 1572872 | tf_op jit(solution)/shard_map/while/body/eval_jaxpr/ppermute | solution.py:14
  278.9 23.8 %collective-permute-start = (f32[256,512]{1,0:T(8,128)S(1)}, f32[256,512]{1,0:T(8,128)}, u32[]{:S(2)}, u32[]{:S(2)}) collective-permute-start(f32[256,512]{1,0:T(8,128)S(1)} %get-tuple-element.431), channel_id=1, source_target_pairs={{0,8},{8,16},{16,24},{1,9},{9,17},{17,25},{2,10},{10,18},{18,26},{... | collective-permute-start | bytes 1572872 | tf_op jit(solution)/shard_map/while/body/eval_jaxpr/ppermute | solution.py:14
  291.2 18.2 %collective-permute-start.1 = (f32[512,256]{1,0:T(8,128)S(1)}, f32[512,256]{1,0:T(8,128)}, u32[]{:S(2)}, u32[]{:S(2)}) collective-permute-start(f32[512,256]{1,0:T(8,128)S(1)} %get-tuple-element.432), channel_id=1, source_target_pairs={{0,8},{8,16},{16,24},{1,9},{9,17},{17,25},{2,10},{10,18},{18,26},{... | collective-permute-start | bytes 1572872 | tf_op jit(solution)/shard_map/while/body/eval_jaxpr/ppermute | solution.py:14
  328.7 13.6 %collective-permute-start = (f32[256,512]{1,0:T(8,128)S(1)}, f32[256,512]{1,0:T(8,128)}, u32[]{:S(2)}, u32[]{:S(2)}) collective-permute-start(f32[256,512]{1,0:T(8,128)S(1)} %get-tuple-element.431), channel_id=1, source_target_pairs={{0,8},{8,16},{16,24},{1,9},{9,17},{17,25},{2,10},{10,18},{18,26},{... | collective-permute-start | bytes 1572872 | tf_op jit(solution)/shard_map/while/body/eval_jaxpr/ppermute | solution.py:14
  330.7 17.6 %collective-permute-start.1 = (f32[512,256]{1,0:T(8,128)S(1)}, f32[512,256]{1,0:T(8,128)}, u32[]{:S(2)}, u32[]{:S(2)}) collective-permute-start(f32[512,256]{1,0:T(8,128)S(1)} %get-tuple-element.432), channel_id=1, source_target_pairs={{0,8},{8,16},{16,24},{1,9},{9,17},{17,25},{2,10},{10,18},{18,26},{... | collective-permute-start | bytes 1572872 | tf_op jit(solution)/shard_map/while/body/eval_jaxpr/ppermute | solution.py:14
  350.7 34.6 %collective-permute-start = (f32[256,512]{1,0:T(8,128)S(1)}, f32[256,512]{1,0:T(8,128)}, u32[]{:S(2)}, u32[]{:S(2)}) collective-permute-start(f32[256,512]{1,0:T(8,128)S(1)} %get-tuple-element.431), channel_id=1, source_target_pairs={{0,8},{8,16},{16,24},{1,9},{9,17},{17,25},{2,10},{10,18},{18,26},{... | collective-permute-start | bytes 1572872 | tf_op jit(solution)/shard_map/while/body/eval_jaxpr/ppermute | solution.py:14
  374.2 16.7 %collective-permute-start.1 = (f32[512,256]{1,0:T(8,128)S(1)}, f32[512,256]{1,0:T(8,128)}, u32[]{:S(2)}, u32[]{:S(2)}) collective-permute-start(f32[512,256]{1,0:T(8,128)S(1)} %get-tuple-element.432), channel_id=1, source_target_pairs={{0,8},{8,16},{16,24},{1,9},{9,17},{17,25},{2,10},{10,18},{18,26},{... | collective-permute-start | bytes 1572872 | tf_op jit(solution)/shard_map/while/body/eval_jaxpr/ppermute | solution.py:14
  393.2 27.3 %collective-permute-start = (f32[256,512]{1,0:T(8,128)S(1)}, f32[256,512]{1,0:T(8,128)}, u32[]{:S(2)}, u32[]{:S(2)}) collective-permute-start(f32[256,512]{1,0:T(8,128)S(1)} %get-tuple-element.431), channel_id=1, source_target_pairs={{0,8},{8,16},{16,24},{1,9},{9,17},{17,25},{2,10},{10,18},{18,26},{... | collective-permute-start | bytes 1572872 | tf_op jit(solution)/shard_map/while/body/eval_jaxpr/ppermute | solution.py:14
  398.5 26.0 %collective-permute-start.1 = (f32[512,256]{1,0:T(8,128)S(1)}, f32[512,256]{1,0:T(8,128)}, u32[]{:S(2)}, u32[]{:S(2)}) collective-permute-start(f32[512,256]{1,0:T(8,128)S(1)} %get-tuple-element.432), channel_id=1, source_target_pairs={{0,8},{8,16},{16,24},{1,9},{9,17},{17,25},{2,10},{10,18},{18,26},{... | collective-permute-start | bytes 1572872 | tf_op jit(solution)/shard_map/while/body/eval_jaxpr/ppermute | solution.py:14
  426.8 20.7 %collective-permute-start = (f32[256,512]{1,0:T(8,128)S(1)}, f32[256,512]{1,0:T(8,128)}, u32[]{:S(2)}, u32[]{:S(2)}) collective-permute-start(f32[256,512]{1,0:T(8,128)S(1)} %get-tuple-element.431), channel_id=1, source_target_pairs={{0,8},{8,16},{16,24},{1,9},{9,17},{17,25},{2,10},{10,18},{18,26},{... | collective-permute-start | bytes 1572872 | tf_op jit(solution)/shard_map/while/body/eval_jaxpr/ppermute | solution.py:14
  437.9 15.3 %collective-permute-start.1 = (f32[512,256]{1,0:T(8,128)S(1)}, f32[512,256]{1,0:T(8,128)}, u32[]{:S(2)}, u32[]{:S(2)}) collective-permute-start(f32[512,256]{1,0:T(8,128)S(1)} %get-tuple-element.432), channel_id=1, source_target_pairs={{0,8},{8,16},{16,24},{1,9},{9,17},{17,25},{2,10},{10,18},{18,26},{... | collective-permute-start | bytes 1572872 | tf_op jit(solution)/shard_map/while/body/eval_jaxpr/ppermute | solution.py:14
  453.1 19.9 %copy-start.10 = (bf16[2,512,256]{2,1,0:T(8,128)(2,1)S(1)}, bf16[2,512,256]{2,1,0:T(8,128)(2,1)}, u32[]{:S(2)}) copy-start(bf16[2,512,256]{2,1,0:T(8,128)(2,1)} %copy-done.9) | copy-start | bytes 1572868
  453.1 22.9 %copy-start.13 = (bf16[2,2560,256]{2,1,0:T(8,128)(2,1)S(1)}, bf16[2,2560,256]{2,1,0:T(8,128)(2,1)}, u32[]{:S(2)}) copy-start(bf16[2,2560,256]{2,1,0:T(8,128)(2,1)} %broadcast_dynamic-update-slice_fusion) | copy-start | bytes 7864324
  454.8 21.3 %collective-permute-start.7 = (bf16[2,512,256]{2,1,0:T(8,128)(2,1)}, bf16[2,512,256]{2,1,0:T(8,128)(2,1)S(1)}, u32[]{:S(2)}, u32[]{:S(2)}) collective-permute-start(bf16[2,512,256]{2,1,0:T(8,128)(2,1)} %collective-permute-done.6), channel_id=1, source_target_pairs={{0,8},{8,16},{16,24},{1,9},{9,17},{17,25},{2,10},{10,18},{18,26},{... | collective-permute-start | bytes 1572872 | tf_op jit(solution)/shard_map/ppermute | solution.py:14
  473.9 5.9 copy-start.12
  485.5 8.3 %copy-start.5 = (bf16[1,256,4096]{2,1,0:T(8,128)(2,1)S(1)}, bf16[1,256,4096]{2,1,0:T(8,128)(2,1)}, u32[]{:S(2)}) copy-start(bf16[1,256,4096]{2,1,0:T(8,128)(2,1)} %param.19) | copy-start | bytes 6291460
  601.8 6.2 %copy-start.1 = (bf16[4096,1]{0,1:T(2,128)(2,1)S(1)}, bf16[4096,1]{0,1:T(2,128)(2,1)}, u32[]{:S(2)}) copy-start(bf16[4096,1]{0,1:T(2,128)(2,1)} %param.14) | copy-start | bytes 24580
  (9 other events, 38.8 us)
Sparse Core Ops, SparseCore 0:
  8.9 84.7 all-gather.2
  494.0 77.1 all-gather.4
where the time goes:
time: 617 us; the launch traced here: 615 us
  starting transfers between devices  185 us (30%)
  waiting for transfers between devices  181 us (29%)
  blocking collectives  65.8 us (11%)
  matrix products  65.7 us (11%)
  other arithmetic  60.9 us (10%)
  local copies, waits for them, and re-layouts  38.9 us (6%)
  between operations  14.3 us (2%)
    ppermute x22, starting transfers between devices, shifted(): return lax.ppermute(block, axis, route)  185 us
    ppermute x22, waiting for transfers between devices, shifted(): return lax.ppermute(block, axis, route)  93.9 us
    all_gather x1, waiting for transfers between devices, body(): piece = lax.all_gather(flattened, 'head', axis=1, tiled=True)  86.4 us
    all_to_all x1, blocking collectives, body(): lax.all_to_all(final_mixing_matrix, 'head', split_axis=2, concat_axis=0,...  65.8 us
    unnamed x45, local copies, waits for them, and re-layouts  31.9 us
    unnamed x1, other arithmetic  21.6 us
    select_n x8, other arithmetic, turn(): fast_all = jnp.where(live, stored, fast_all)  15.2 us
  transfers between devices with their start and end apart: 24, of which 19 were waited for; matrix products, arithmetic and copies ran while one was open for 20% of the time, Pallas kernels for 0%

commit v1 on v0

--- a/solution.py
+++ b/solution.py
@@ -163,7 +163,12 @@
     head_out = combine(attended_output, carried[2], adapter_gain_vector[0]).reshape(
         total_rows, head_dim
     )
-    columns = lax.all_to_all(final_mixing_matrix, "head", split_axis=2, concat_axis=0, tiled=True)
+    columns = jnp.concatenate(
+        lax.all_to_all(
+            jnp.stack(jnp.split(final_mixing_matrix, lax.axis_size("head"), axis=2)), "head", 0, 0
+        ),
+        axis=0,
+    )
     columns = columns.reshape(-1, columns.shape[2])
     result = jnp.dot(
         lax.all_gather(head_out, "head", axis=1, tiled=True),

time: 617 us -> 594 us (0.963)
  other arithmetic: 60.9 us -> 30.8 us
  local copies, waits for them, and re-layouts: 38.9 us -> 18.7 us
  blocking collectives: 65.8 us -> 85.2 us
  waiting for transfers between devices: 181 us -> 191 us
    unnamed x1 -> x0, other arithmetic: 21.6 us -> none
    all_to_all x1, blocking collectives: 65.8 us -> 85.2 us  [body(): lax.all_to_all(jnp.stack(jnp.split(final_mixing_matrix, lax.axis_size('he...]
    unnamed x45 -> x47, local copies, waits for them, and re-layouts: 31.9 us -> 12.8 us
    ppermute x22, waiting for transfers between devices: 93.9 us -> 103 us  [shifted(): return lax.ppermute(block, axis, route)]
    select_n x8, other arithmetic: 9.06 us -> 0.66 us  [turn(): use_in = jnp.where(token_position == 0, start_in, held_in)]
  transfers between devices with their start and end apart: 24 -> 24, of which waited for: 19 -> 20; matrix products, arithmetic and copies ran while one was open for 20% -> 13% of each run, Pallas kernels for 0% -> 0%
where the time goes in v1:
time: 594 us; the launch traced here: 586 us
  waiting for transfers between devices  191 us (32%)
  starting transfers between devices  179 us (30%)
  blocking collectives  85.2 us (14%)
  matrix products  64.3 us (11%)
  other arithmetic  30.8 us (5%)
  local copies, waits for them, and re-layouts  18.7 us (3%)
  between operations  14.3 us (2%)
    ppermute x22, starting transfers between devices, shifted(): return lax.ppermute(block, axis, route)  179 us
    ppermute x22, waiting for transfers between devices, shifted(): return lax.ppermute(block, axis, route)  103 us
    all_gather x1, waiting for transfers between devices, body(): piece = lax.all_gather(flattened, 'head', axis=1, tiled=True)  86.4 us
    all_to_all x1, blocking collectives, body(): lax.all_to_all(jnp.stack(jnp.split(final_mixing_matrix, lax.axis_size('he...  85.2 us
    select_n x8, other arithmetic, turn(): fast_all = jnp.where(live, stored, fast_all)  15.3 us
    unnamed x47, local copies, waits for them, and re-layouts  12.8 us
  transfers between devices with their start and end apart: 24, of which 20 were waited for; matrix products, arithmetic and copies ran while one was open for 13% of the time, Pallas kernels for 0%

profile of v1, /device:TPU:0, one launch (start us, length us, event | category | flops | bytes accessed | tf_op | source)
XLA Modules:
  0.0 586.5 jit_solution(16104880725078889459)
XLA Ops:
  7.3 86.4 %all-gather.3.cloned.1.call-done = bf16[1024,4096]{1,0:T(8,128)(2,1)} async-done(((bf16[1024,512]{1,0:T(8,128)(2,1)}), bf16[1024,4096]{1,0:T(8,128)(2,1)}) %all-gather.3.cloned.1.call-update) | async-done | bytes 8388624 | tf_op jit(solution)/shard_map/all_gather | solution.py:109
  93.7 11.0 %fusion.61 = f32[1024,768]{1,0:T(8,128)S(1)} fusion(bf16[1024,4096]{1,0:T(8,128)(2,1)} %all-gather.3.cloned.1.call-done, bf16[4096,1,768]{2,0,1:T(8,128)(2,1)} %param.13), kind=kOutput, calls=%fused_computation.72 | convolution fusion | flops 6442450944 | bytes 17825792 | tf_op jit(solution)/shard_map/dot_general | solution.py:110
  136.2 5.3 collective-permute-start.6
  141.5 5.9 %collective-permute-done.3 = bf16[2,512,256]{2,1,0:T(8,128)(2,1)} collective-permute-done((bf16[2,512,256]{2,1,0:T(8,128)(2,1)S(1)}, bf16[2,512,256]{2,1,0:T(8,128)(2,1)}, u32[]{:S(2)}, u32[]{:S(2)}) %collective-permute-start.3) | collective-permute-done | bytes 524320 | tf_op jit(solution)/shard_map/ppermute | solution.py:14
  147.4 5.3 collective-permute-start.4
  153.8 292.6 %while.19 = (s32[]{:T(128)}, f32[256,512]{1,0:T(8,128)}, f32[512,256]{1,0:T(8,128)S(1)}, f32[2,512,256]{2,1,0:T(8,128)}, s32[]{:T(128)}, /*index=5*/pred[]{:T(51...) while((s32[]{:T(128)}, f32[256,512]{1,0:T(8,128)}, ...), condition=%wide.region_9.10_spmd, body=%wide.region_4.9_spmd.sunk | while | flops 5647237120 | bytes 39062676 | solution.py:162
  155.0 17.6 %conditional.2 = (f32[256,512]{1,0:T(8,128)S(1)}, f32[512,256]{1,0:T(8,128)S(1)}, f32[1,512,256]{2,1,0:T(8,128)S(1)}) conditional(s32[]{:T(128)} %convert_element_type.110, (f32[256,512]{1,0:T(8,128)S(1)}, f32[512,256]{1,0:T(8,128)S(1)}) %tuple.60, (bf16[2,512,256]{2,1,0:T(8,128)(2,1)}, s32[]{:T(128)}, bf16[2,512,256]{2,1,0:T(8,128)(2,1)}, ...), branch_computations={%region_5.5_spmd, %region_6.8_spmd} | conditional | flops 5646843904 | bytes 28051632 | solution.py:154
  177.9 8.3 %collective-permute-done = f32[256,512]{1,0:T(8,128)} collective-permute-done((f32[256,512]{1,0:T(8,128)S(1)}, f32[256,512]{1,0:T(8,128)}, u32[]{:S(2)}, u32[]{:S(2)}) %collective-permute-start) | collective-permute-done | bytes 524320 | tf_op jit(solution)/shard_map/while/body/eval_jaxpr/ppermute | solution.py:14
  186.2 9.0 %collective-permute-done.1 = f32[512,256]{1,0:T(8,128)S(1)} collective-permute-done((f32[512,256]{1,0:T(8,128)}, f32[512,256]{1,0:T(8,128)S(1)}, u32[]{:S(2)}, u32[]{:S(2)}) %collective-permute-start.1) | collective-permute-done | bytes 524320 | tf_op jit(solution)/shard_map/while/body/eval_jaxpr/ppermute | solution.py:14
  196.5 22.6 %collective-permute-start = (f32[256,512]{1,0:T(8,128)S(1)}, f32[256,512]{1,0:T(8,128)}, u32[]{:S(2)}, u32[]{:S(2)}) collective-permute-start(f32[256,512]{1,0:T(8,128)S(1)} %get-tuple-element.431), channel_id=1, source_target_pairs={{0,8},{8,16},{16,24},{1,9},{9,17},{17,25},{2,10},{10,18},{18,26},{... | collective-permute-start | bytes 1572872 | tf_op jit(solution)/shard_map/while/body/eval_jaxpr/ppermute | solution.py:14
  222.3 8.3 %collective-permute-done = f32[256,512]{1,0:T(8,128)} collective-permute-done((f32[256,512]{1,0:T(8,128)S(1)}, f32[256,512]{1,0:T(8,128)}, u32[]{:S(2)}, u32[]{:S(2)}) %collective-permute-start) | collective-permute-done | bytes 524320 | tf_op jit(solution)/shard_map/while/body/eval_jaxpr/ppermute | solution.py:14
  230.6 8.1 %collective-permute-done.1 = f32[512,256]{1,0:T(8,128)S(1)} collective-permute-done((f32[512,256]{1,0:T(8,128)}, f32[512,256]{1,0:T(8,128)S(1)}, u32[]{:S(2)}, u32[]{:S(2)}) %collective-permute-start.1) | collective-permute-done | bytes 524320 | tf_op jit(solution)/shard_map/while/body/eval_jaxpr/ppermute | solution.py:14
  240.0 5.1 collective-permute-start
  245.1 19.8 %collective-permute-start.1 = (f32[512,256]{1,0:T(8,128)}, f32[512,256]{1,0:T(8,128)S(1)}, u32[]{:S(2)}, u32[]{:S(2)}) collective-permute-start(f32[512,256]{1,0:T(8,128)} %copy-done.5), channel_id=1, source_target_pairs={{0,8},{8,16},{16,24},{1,9},{9,17},{17,25},{2,10},{10,18},{18,26},{... | collective-permute-start | bytes 1572872 | tf_op jit(solution)/shard_map/while/body/eval_jaxpr/ppermute | solution.py:14
  266.9 6.6 %collective-permute-done.1 = f32[512,256]{1,0:T(8,128)S(1)} collective-permute-done((f32[512,256]{1,0:T(8,128)}, f32[512,256]{1,0:T(8,128)S(1)}, u32[]{:S(2)}, u32[]{:S(2)}) %collective-permute-start.1) | collective-permute-done | bytes 524320 | tf_op jit(solution)/shard_map/while/body/eval_jaxpr/ppermute | solution.py:14
  274.8 12.1 %collective-permute-start = (f32[256,512]{1,0:T(8,128)S(1)}, f32[256,512]{1,0:T(8,128)}, u32[]{:S(2)}, u32[]{:S(2)}) collective-permute-start(f32[256,512]{1,0:T(8,128)S(1)} %get-tuple-element.431), channel_id=1, source_target_pairs={{0,8},{8,16},{16,24},{1,9},{9,17},{17,25},{2,10},{10,18},{18,26},{... | collective-permute-start | bytes 1572872 | tf_op jit(solution)/shard_map/while/body/eval_jaxpr/ppermute | solution.py:14
  293.2 5.2 collective-permute-done
  298.4 6.7 %collective-permute-done.1 = f32[512,256]{1,0:T(8,128)S(1)} collective-permute-done((f32[512,256]{1,0:T(8,128)}, f32[512,256]{1,0:T(8,128)S(1)}, u32[]{:S(2)}, u32[]{:S(2)}) %collective-permute-start.1) | collective-permute-done | bytes 524320 | tf_op jit(solution)/shard_map/while/body/eval_jaxpr/ppermute | solution.py:14
  306.3 17.6 %conditional.2 = (f32[256,512]{1,0:T(8,128)S(1)}, f32[512,256]{1,0:T(8,128)S(1)}, f32[1,512,256]{2,1,0:T(8,128)S(1)}) conditional(s32[]{:T(128)} %convert_element_type.110, (f32[256,512]{1,0:T(8,128)S(1)}, f32[512,256]{1,0:T(8,128)S(1)}) %tuple.60, (bf16[2,512,256]{2,1,0:T(8,128)(2,1)}, s32[]{:T(128)}, bf16[2,512,256]{2,1,0:T(8,128)(2,1)}, ...), branch_computations={%region_5.5_spmd, %region_6.8_spmd} | conditional | flops 5646843904 | bytes 28051632 | solution.py:154
  337.5 6.1 %collective-permute-done.1 = f32[512,256]{1,0:T(8,128)S(1)} collective-permute-done((f32[512,256]{1,0:T(8,128)}, f32[512,256]{1,0:T(8,128)S(1)}, u32[]{:S(2)}, u32[]{:S(2)}) %collective-permute-start.1) | collective-permute-done | bytes 524320 | tf_op jit(solution)/shard_map/while/body/eval_jaxpr/ppermute | solution.py:14
  345.0 23.8 %collective-permute-start = (f32[256,512]{1,0:T(8,128)S(1)}, f32[256,512]{1,0:T(8,128)}, u32[]{:S(2)}, u32[]{:S(2)}) collective-permute-start(f32[256,512]{1,0:T(8,128)S(1)} %get-tuple-element.431), channel_id=1, source_target_pairs={{0,8},{8,16},{16,24},{1,9},{9,17},{17,25},{2,10},{10,18},{18,26},{... | collective-permute-start | bytes 1572872 | tf_op jit(solution)/shard_map/while/body/eval_jaxpr/ppermute | solution.py:14
  372.0 7.8 %collective-permute-done = f32[256,512]{1,0:T(8,128)} collective-permute-done((f32[256,512]{1,0:T(8,128)S(1)}, f32[256,512]{1,0:T(8,128)}, u32[]{:S(2)}, u32[]{:S(2)}) %collective-permute-start) | collective-permute-done | bytes 524320 | tf_op jit(solution)/shard_map/while/body/eval_jaxpr/ppermute | solution.py:14
  379.8 5.7 collective-permute-done.1
  386.8 5.1 collective-permute-start
  392.0 19.8 %collective-permute-start.1 = (f32[512,256]{1,0:T(8,128)}, f32[512,256]{1,0:T(8,128)S(1)}, u32[]{:S(2)}, u32[]{:S(2)}) collective-permute-start(f32[512,256]{1,0:T(8,128)} %copy-done.5), channel_id=1, source_target_pairs={{0,8},{8,16},{16,24},{1,9},{9,17},{17,25},{2,10},{10,18},{18,26},{... | collective-permute-start | bytes 1572872 | tf_op jit(solution)/shard_map/while/body/eval_jaxpr/ppermute | solution.py:14
  420.0 10.9 %collective-permute-start = (f32[256,512]{1,0:T(8,128)S(1)}, f32[256,512]{1,0:T(8,128)}, u32[]{:S(2)}, u32[]{:S(2)}) collective-permute-start(f32[256,512]{1,0:T(8,128)S(1)} %get-tuple-element.431), channel_id=1, source_target_pairs={{0,8},{8,16},{16,24},{1,9},{9,17},{17,25},{2,10},{10,18},{18,26},{... | collective-permute-start | bytes 1572872 | tf_op jit(solution)/shard_map/while/body/eval_jaxpr/ppermute | solution.py:14
  440.7 5.7 collective-permute-done.1
  448.0 15.0 %collective-permute-start.7 = (bf16[2,512,256]{2,1,0:T(8,128)(2,1)}, bf16[2,512,256]{2,1,0:T(8,128)(2,1)S(1)}, u32[]{:S(2)}, u32[]{:S(2)}) collective-permute-start(bf16[2,512,256]{2,1,0:T(8,128)(2,1)} %collective-permute-done.6), channel_id=1, source_target_pairs={{0,8},{8,16},{16,24},{1,9},{9,17},{17,25},{2,10},{10,18},{18,26},{... | collective-permute-start | bytes 1572872 | tf_op jit(solution)/shard_map/ppermute | solution.py:14
  473.5 5.6 fusion.81
  479.2 8.3 %fusion.70 = bf16[2,512,256]{2,1,0:T(8,128)(2,1)} fusion(bf16[2,2560,256]{2,1,0:T(8,128)(2,1)} %copy-done.17, f32[2,512]{1,0:T(2,128)S(1)} %fusion.81, f32[2,512,256]{2,1,0:T(8,128)S(1)} %copy-done.1, f32[256]{0:T(256)S(1)} %bitcast.95, f32[2,512]{1,0:T(2,128)S(1)} %add_rsqrt_fusion, f32[]{:T(128)} %bitcast.83, pred[512,2560]{1,0:T(8,128)(4,1)} %fusion.67, ...), kind=kOutput, calls=%fused_computation.84 | convolution fusion | flops 2698513920 | bytes 8659972 | tf_op jit(solution)/shard_map/sqk,skd->sqd/dot_general | solution.py:84
  487.7 85.2 %all_to_all.5 = bf16[8,1,256,512]{3,2,1,0:T(8,128)(2,1)S(1)} all-to-all(bf16[8,1,256,512]{3,2,1,0:T(8,128)(2,1)S(1)} %bitcast_dynamic-update-slice_fusion), channel_id=1, replica_groups=mesh['seq'=4,'head'=8] {'head'}, dimensions={0} | all-to-all | bytes 4194304 | tf_op jit(solution)/shard_map/all_to_all | solution.py:167
  574.2 5.5 convolution_convert_fusion
  (190 shorter events, 139.4 us)
Async XLA Ops:
  6.5 98.6 %copy-start = (bf16[4096,1]{0,1:T(2,128)(2,1)S(1)}, bf16[4096,1]{0,1:T(2,128)(2,1)}, u32[]{:S(2)}) copy-start(bf16[4096,1]{0,1:T(2,128)(2,1)} %param.14) | copy-start | bytes 24580
  6.5 87.2 %all-gather.3.cloned.1.call-start = ((), (), s32[]{:S(2)}) async-start(), calls=%async_computation.1 | async-start | bytes 9437184 | tf_op jit(solution)/shard_map/all_gather | solution.py:109
  7.3 566.9 %all-gather.5.cloned.1.call-start = ((), (), s32[]{:S(2)}) async-start(), calls=%async_computation.2 | async-start | bytes 4718592 | tf_op jit(solution)/shard_map/all_gather | solution.py:174
  93.7 11.4 %copy-start.6 = (bf16[1024,4096]{1,0:T(8,128)(2,1)S(1)}, bf16[1024,4096]{1,0:T(8,128)(2,1)}, u32[]{:S(2)}) copy-start(bf16[1024,4096]{1,0:T(8,128)(2,1)} %all-gather.3.cloned.1.call-done) | copy-start | bytes 25165828
  109.1 16.0 %collective-permute-start.2 = (bf16[2,512,256]{2,1,0:T(8,128)(2,1)}, bf16[2,512,256]{2,1,0:T(8,128)(2,1)S(1)}, u32[]{:S(2)}, u32[]{:S(2)}) collective-permute-start(bf16[2,512,256]{2,1,0:T(8,128)(2,1)} %bitcast.8), channel_id=1, source_target_pairs={{0,8},{8,16},{16,24},{1,9},{9,17},{17,25},{2,10},{10,18},{18,26},{... | collective-permute-start | bytes 1572872 | tf_op jit(solution)/shard_map/ppermute | solution.py:14
  118.8 17.4 %collective-permute-start.5 = (bf16[2,512,256]{2,1,0:T(8,128)(2,1)S(1)}, bf16[2,512,256]{2,1,0:T(8,128)(2,1)}, u32[]{:S(2)}, u32[]{:S(2)}) collective-permute-start(bf16[2,512,256]{2,1,0:T(8,128)(2,1)S(1)} %bitcast.88), channel_id=1, source_target_pairs={{0,8},{8,16},{16,24},{1,9},{9,17},{17,25},{2,10},{10,18},{18,26},{... | collective-permute-start | bytes 1572872 | tf_op jit(solution)/shard_map/ppermute | solution.py:14
  125.1 28.7 %copy-start.12 = (bf16[2,512,256]{2,1,0:T(8,128)(2,1)}, bf16[2,512,256]{2,1,0:T(8,128)(2,1)S(1)}, u32[]{:S(2)}) copy-start(bf16[2,512,256]{2,1,0:T(8,128)(2,1)S(1)} %collective-permute-done.2) | copy-start | bytes 1572868
  125.1 22.4 %collective-permute-start.3 = (bf16[2,512,256]{2,1,0:T(8,128)(2,1)S(1)}, bf16[2,512,256]{2,1,0:T(8,128)(2,1)}, u32[]{:S(2)}, u32[]{:S(2)}) collective-permute-start(bf16[2,512,256]{2,1,0:T(8,128)(2,1)S(1)} %collective-permute-done.2), channel_id=1, source_target_pairs={{0,8},{8,16},{16,24},{1,9},{9,17},{17,25},{2,10},{10,18},{18,26},{... | collective-permute-start | bytes 1572872 | tf_op jit(solution)/shard_map/ppermute | solution.py:14
  136.2 311.8 %collective-permute-start.6 = (bf16[2,512,256]{2,1,0:T(8,128)(2,1)}, bf16[2,512,256]{2,1,0:T(8,128)(2,1)}, u32[]{:S(2)}, u32[]{:S(2)}) collective-permute-start(bf16[2,512,256]{2,1,0:T(8,128)(2,1)} %collective-permute-done.5), channel_id=1, source_target_pairs={{0,8},{8,16},{16,24},{1,9},{9,17},{17,25},{2,10},{10,18},{18,26},{... | collective-permute-start | bytes 1572872 | tf_op jit(solution)/shard_map/ppermute | solution.py:14
  147.4 315.6 %collective-permute-start.4 = (bf16[2,512,256]{2,1,0:T(8,128)(2,1)}, bf16[2,512,256]{2,1,0:T(8,128)(2,1)}, u32[]{:S(2)}, u32[]{:S(2)}) collective-permute-start(bf16[2,512,256]{2,1,0:T(8,128)(2,1)} %collective-permute-done.3), channel_id=1, source_target_pairs={{0,8},{8,16},{16,24},{1,9},{9,17},{17,25},{2,10},{10,18},{18,26},{... | collective-permute-start | bytes 1572872 | tf_op jit(solution)/shard_map/ppermute | solution.py:14
  172.6 13.6 %collective-permute-start = (f32[256,512]{1,0:T(8,128)S(1)}, f32[256,512]{1,0:T(8,128)}, u32[]{:S(2)}, u32[]{:S(2)}) collective-permute-start(f32[256,512]{1,0:T(8,128)S(1)} %get-tuple-element.431), channel_id=1, source_target_pairs={{0,8},{8,16},{16,24},{1,9},{9,17},{17,25},{2,10},{10,18},{18,26},{... | collective-permute-start | bytes 1572872 | tf_op jit(solution)/shard_map/while/body/eval_jaxpr/ppermute | solution.py:14
  174.7 20.5 %collective-permute-start.1 = (f32[512,256]{1,0:T(8,128)}, f32[512,256]{1,0:T(8,128)S(1)}, u32[]{:S(2)}, u32[]{:S(2)}) collective-permute-start(f32[512,256]{1,0:T(8,128)} %copy-done.5), channel_id=1, source_target_pairs={{0,8},{8,16},{16,24},{1,9},{9,17},{17,25},{2,10},{10,18},{18,26},{... | collective-permute-start | bytes 1572872 | tf_op jit(solution)/shard_map/while/body/eval_jaxpr/ppermute | solution.py:14
  196.5 22.6 %copy-start.5 = (f32[512,256]{1,0:T(8,128)}, f32[512,256]{1,0:T(8,128)S(1)}, u32[]{:S(2)}) copy-start(f32[512,256]{1,0:T(8,128)S(1)} %get-tuple-element.432) | copy-start | bytes 1572868 | tf_op jit(solution)/shard_map/while
  196.5 34.1 %collective-permute-start = (f32[256,512]{1,0:T(8,128)S(1)}, f32[256,512]{1,0:T(8,128)}, u32[]{:S(2)}, u32[]{:S(2)}) collective-permute-start(f32[256,512]{1,0:T(8,128)S(1)} %get-tuple-element.431), channel_id=1, source_target_pairs={{0,8},{8,16},{16,24},{1,9},{9,17},{17,25},{2,10},{10,18},{18,26},{... | collective-permute-start | bytes 1572872 | tf_op jit(solution)/shard_map/while/body/eval_jaxpr/ppermute | solution.py:14
  219.1 19.6 %collective-permute-start.1 = (f32[512,256]{1,0:T(8,128)}, f32[512,256]{1,0:T(8,128)S(1)}, u32[]{:S(2)}, u32[]{:S(2)}) collective-permute-start(f32[512,256]{1,0:T(8,128)} %copy-done.5), channel_id=1, source_target_pairs={{0,8},{8,16},{16,24},{1,9},{9,17},{17,25},{2,10},{10,18},{18,26},{... | collective-permute-start | bytes 1572872 | tf_op jit(solution)/shard_map/while/body/eval_jaxpr/ppermute | solution.py:14
  240.0 26.8 %collective-permute-start = (f32[256,512]{1,0:T(8,128)S(1)}, f32[256,512]{1,0:T(8,128)}, u32[]{:S(2)}, u32[]{:S(2)}) collective-permute-start(f32[256,512]{1,0:T(8,128)S(1)} %get-tuple-element.431), channel_id=1, source_target_pairs={{0,8},{8,16},{16,24},{1,9},{9,17},{17,25},{2,10},{10,18},{18,26},{... | collective-permute-start | bytes 1572872 | tf_op jit(solution)/shard_map/while/body/eval_jaxpr/ppermute | solution.py:14
  245.1 28.3 %collective-permute-start.1 = (f32[512,256]{1,0:T(8,128)}, f32[512,256]{1,0:T(8,128)S(1)}, u32[]{:S(2)}, u32[]{:S(2)}) collective-permute-start(f32[512,256]{1,0:T(8,128)} %copy-done.5), channel_id=1, source_target_pairs={{0,8},{8,16},{16,24},{1,9},{9,17},{17,25},{2,10},{10,18},{18,26},{... | collective-permute-start | bytes 1572872 | tf_op jit(solution)/shard_map/while/body/eval_jaxpr/ppermute | solution.py:14
  274.8 12.1 %copy-start.5 = (f32[512,256]{1,0:T(8,128)}, f32[512,256]{1,0:T(8,128)S(1)}, u32[]{:S(2)}) copy-start(f32[512,256]{1,0:T(8,128)S(1)} %get-tuple-element.432) | copy-start | bytes 1572868 | tf_op jit(solution)/shard_map/while
  274.8 23.6 %collective-permute-start = (f32[256,512]{1,0:T(8,128)S(1)}, f32[256,512]{1,0:T(8,128)}, u32[]{:S(2)}, u32[]{:S(2)}) collective-permute-start(f32[256,512]{1,0:T(8,128)S(1)} %get-tuple-element.431), channel_id=1, source_target_pairs={{0,8},{8,16},{16,24},{1,9},{9,17},{17,25},{2,10},{10,18},{18,26},{... | collective-permute-start | bytes 1572872 | tf_op jit(solution)/shard_map/while/body/eval_jaxpr/ppermute | solution.py:14
  286.9 18.2 %collective-permute-start.1 = (f32[512,256]{1,0:T(8,128)}, f32[512,256]{1,0:T(8,128)S(1)}, u32[]{:S(2)}, u32[]{:S(2)}) collective-permute-start(f32[512,256]{1,0:T(8,128)} %copy-done.5), channel_id=1, source_target_pairs={{0,8},{8,16},{16,24},{1,9},{9,17},{17,25},{2,10},{10,18},{18,26},{... | collective-permute-start | bytes 1572872 | tf_op jit(solution)/shard_map/while/body/eval_jaxpr/ppermute | solution.py:14
  323.9 13.6 %collective-permute-start = (f32[256,512]{1,0:T(8,128)S(1)}, f32[256,512]{1,0:T(8,128)}, u32[]{:S(2)}, u32[]{:S(2)}) collective-permute-start(f32[256,512]{1,0:T(8,128)S(1)} %get-tuple-element.431), channel_id=1, source_target_pairs={{0,8},{8,16},{16,24},{1,9},{9,17},{17,25},{2,10},{10,18},{18,26},{... | collective-permute-start | bytes 1572872 | tf_op jit(solution)/shard_map/while/body/eval_jaxpr/ppermute | solution.py:14
  326.0 17.6 %collective-permute-start.1 = (f32[512,256]{1,0:T(8,128)}, f32[512,256]{1,0:T(8,128)S(1)}, u32[]{:S(2)}, u32[]{:S(2)}) collective-permute-start(f32[512,256]{1,0:T(8,128)} %copy-done.5), channel_id=1, source_target_pairs={{0,8},{8,16},{16,24},{1,9},{9,17},{17,25},{2,10},{10,18},{18,26},{... | collective-permute-start | bytes 1572872 | tf_op jit(solution)/shard_map/while/body/eval_jaxpr/ppermute | solution.py:14
  345.0 23.8 %copy-start.5 = (f32[512,256]{1,0:T(8,128)}, f32[512,256]{1,0:T(8,128)S(1)}, u32[]{:S(2)}) copy-start(f32[512,256]{1,0:T(8,128)S(1)} %get-tuple-element.432) | copy-start | bytes 1572868 | tf_op jit(solution)/shard_map/while
  345.0 34.8 %collective-permute-start = (f32[256,512]{1,0:T(8,128)S(1)}, f32[256,512]{1,0:T(8,128)}, u32[]{:S(2)}, u32[]{:S(2)}) collective-permute-start(f32[256,512]{1,0:T(8,128)S(1)} %get-tuple-element.431), channel_id=1, source_target_pairs={{0,8},{8,16},{16,24},{1,9},{9,17},{17,25},{2,10},{10,18},{18,26},{... | collective-permute-start | bytes 1572872 | tf_op jit(solution)/shard_map/while/body/eval_jaxpr/ppermute | solution.py:14
  368.7 16.8 %collective-permute-start.1 = (f32[512,256]{1,0:T(8,128)}, f32[512,256]{1,0:T(8,128)S(1)}, u32[]{:S(2)}, u32[]{:S(2)}) collective-permute-start(f32[512,256]{1,0:T(8,128)} %copy-done.5), channel_id=1, source_target_pairs={{0,8},{8,16},{16,24},{1,9},{9,17},{17,25},{2,10},{10,18},{18,26},{... | collective-permute-start | bytes 1572872 | tf_op jit(solution)/shard_map/while/body/eval_jaxpr/ppermute | solution.py:14
  386.8 26.8 %collective-permute-start = (f32[256,512]{1,0:T(8,128)S(1)}, f32[256,512]{1,0:T(8,128)}, u32[]{:S(2)}, u32[]{:S(2)}) collective-permute-start(f32[256,512]{1,0:T(8,128)S(1)} %get-tuple-element.431), channel_id=1, source_target_pairs={{0,8},{8,16},{16,24},{1,9},{9,17},{17,25},{2,10},{10,18},{18,26},{... | collective-permute-start | bytes 1572872 | tf_op jit(solution)/shard_map/while/body/eval_jaxpr/ppermute | solution.py:14
  392.0 26.8 %collective-permute-start.1 = (f32[512,256]{1,0:T(8,128)}, f32[512,256]{1,0:T(8,128)S(1)}, u32[]{:S(2)}, u32[]{:S(2)}) collective-permute-start(f32[512,256]{1,0:T(8,128)} %copy-done.5), channel_id=1, source_target_pairs={{0,8},{8,16},{16,24},{1,9},{9,17},{17,25},{2,10},{10,18},{18,26},{... | collective-permute-start | bytes 1572872 | tf_op jit(solution)/shard_map/while/body/eval_jaxpr/ppermute | solution.py:14
  420.0 20.6 %collective-permute-start = (f32[256,512]{1,0:T(8,128)S(1)}, f32[256,512]{1,0:T(8,128)}, u32[]{:S(2)}, u32[]{:S(2)}) collective-permute-start(f32[256,512]{1,0:T(8,128)S(1)} %get-tuple-element.431), channel_id=1, source_target_pairs={{0,8},{8,16},{16,24},{1,9},{9,17},{17,25},{2,10},{10,18},{18,26},{... | collective-permute-start | bytes 1572872 | tf_op jit(solution)/shard_map/while/body/eval_jaxpr/ppermute | solution.py:14
  431.0 15.4 %collective-permute-start.1 = (f32[512,256]{1,0:T(8,128)}, f32[512,256]{1,0:T(8,128)S(1)}, u32[]{:S(2)}, u32[]{:S(2)}) collective-permute-start(f32[512,256]{1,0:T(8,128)} %copy-done.5), channel_id=1, source_target_pairs={{0,8},{8,16},{16,24},{1,9},{9,17},{17,25},{2,10},{10,18},{18,26},{... | collective-permute-start | bytes 1572872 | tf_op jit(solution)/shard_map/while/body/eval_jaxpr/ppermute | solution.py:14
  446.4 20.4 %copy-start.13 = (bf16[2,512,256]{2,1,0:T(8,128)(2,1)S(1)}, bf16[2,512,256]{2,1,0:T(8,128)(2,1)}, u32[]{:S(2)}) copy-start(bf16[2,512,256]{2,1,0:T(8,128)(2,1)} %copy-done.12) | copy-start | bytes 1572868
  446.4 23.3 %copy-start.16 = (bf16[2,2560,256]{2,1,0:T(8,128)(2,1)S(1)}, bf16[2,2560,256]{2,1,0:T(8,128)(2,1)}, u32[]{:S(2)}) copy-start(bf16[2,2560,256]{2,1,0:T(8,128)(2,1)} %broadcast_dynamic-update-slice_fusion) | copy-start | bytes 7864324
  448.0 21.7 %collective-permute-start.7 = (bf16[2,512,256]{2,1,0:T(8,128)(2,1)}, bf16[2,512,256]{2,1,0:T(8,128)(2,1)S(1)}, u32[]{:S(2)}, u32[]{:S(2)}) collective-permute-start(bf16[2,512,256]{2,1,0:T(8,128)(2,1)} %collective-permute-done.6), channel_id=1, source_target_pairs={{0,8},{8,16},{16,24},{1,9},{9,17},{17,25},{2,10},{10,18},{18,26},{... | collective-permute-start | bytes 1572872 | tf_op jit(solution)/shard_map/ppermute | solution.py:14
  (21 other events, 85.4 us)
Sparse Core Ops, SparseCore 0:
  8.9 84.7 all-gather.2
  487.6 86.5 all-gather.4
